TPU v7x, 128 devices: a whole 4x4x4 slice. The times are simulated.
128 devices in a mesh: seq: 32 (over y, x, core), dp: 4 (over z).
Axes of the slice: x: 4, y: 4, z: 4, core: 2. Of those that a mesh axis runs over, the one named last changes fastest.
Arguments:
- features: bfloat16 [4, 8192, 512], P('dp', 'seq'), may hold values from -6 to 6
- curve_pos: int32 [4, 8192], P('dp'), may hold values from 0 to 8191, as said below
- pattern: int32 [4, 64, 8], P('dp'), may hold values from 0 to 63, as said below
- ln1_gain: float32 [512], replicated, may hold values from 0.5 to 1.5
- w_qkv: bfloat16 [512, 1536], replicated, may hold values from -1 to 1
- w_out: bfloat16 [512, 512], replicated, may hold values from -0.25 to 0.25
- ln2_gain: float32 [512], replicated, may hold values from 0.5 to 1.5
- w_up: bfloat16 [512, 2048], replicated, may hold values from -0.25 to 0.25
- w_down: bfloat16 [2048, 512], replicated, may hold values from -0.125 to 0.125
- out_grad: bfloat16 [4, 8192, 512], P('dp', 'seq'), may hold values from -6 to 6
Outputs:
- block_out: bfloat16 [4, 8192, 512], P('dp', 'seq')
- input_grad: bfloat16 [4, 8192, 512], P('dp', 'seq')
- grad_qkv: float32 [512, 1536], replicated
- grad_out: float32 [512, 512], replicated
- grad_up: float32 [512, 2048], replicated
- grad_down: float32 [2048, 512], replicated
- grad_gain1: float32 [512], replicated
- grad_gain2: float32 [512], replicated
Inputs may be any that keep to these rules, and one draw needn't show every extreme that they name: `curve_pos`: for each tile a permutation of the 8192 curve positions. Of the 256 nodes of one aligned block, at most 16 have positions in one aligned block of 256 curve positions, and in every tile some node block sends exactly 16 to some curve block. `pattern`: each list holds 8 distinct blocks: first the query block q itself, then blocks (q + 2**j) or (q - 2**j) modulo 64.
All inputs are finite; a program needn't handle non-finite values.
Results may differ from a plain program's by a relative error of at most 0.018.
Values may be sent and summed in bfloat16 or wider, within the bound.
A program may use at most 128 MiB of HBM per device.

v0:
```python
from functools import partial
import jax
import jax.numpy as jnp
from jax import lax
from jax.sharding import PartitionSpec as P

D = 512
HEADS = 8
BLK = 128
EPSILON = 1e-05


def from_behind(x, axis, by):
    length = lax.axis_size(axis)
    return lax.ppermute(x, axis, [(i, (i + by) % length) for i in range(length)])


def layer_norm(rows_in, gain_vec):
    values = rows_in.astype(jnp.float32)
    centered = values - jnp.mean(values, axis=-1, keepdims=True)
    inverse = lax.rsqrt(jnp.mean(centered * centered, axis=-1, keepdims=True) + EPSILON)
    normed = centered * inverse
    return ((normed * gain_vec).astype(jnp.bfloat16), normed, inverse)


def norm_back(incoming, gain_vec, normed, inverse):
    scaled = incoming * gain_vec
    return inverse * (
        scaled
        - jnp.mean(scaled, axis=-1, keepdims=True)
        - normed * jnp.mean(scaled * normed, axis=-1, keepdims=True)
    )


def gelu_back(pre_act, incoming):
    return jax.vjp(partial(jax.nn.gelu, approximate=True), pre_act)[1](incoming)[0]


def inner_rows(left_mat, right_mat):
    return lax.dot_general(
        left_mat, right_mat, (((0,), (0,)), ((), ())), preferred_element_type=jnp.float32
    )


def times_transposed(left_mat, right_mat):
    return lax.dot_general(
        left_mat, right_mat, (((1,), (1,)), ((), ())), preferred_element_type=jnp.float32
    )


def split_heads(rows_in):
    return rows_in.reshape(rows_in.shape[0] // BLK, BLK, HEADS, D // HEADS)


def listed_heads(keyval_all, selected):
    blocks = keyval_all.reshape(keyval_all.shape[0] // BLK, BLK, 2 * D)
    picked = blocks[selected]
    shape_out = picked.shape[:3] + (HEADS, D // HEADS)
    return (picked[..., :D].reshape(shape_out), picked[..., D:].reshape(shape_out))


def shift_distances(seq_devices):
    levels = seq_devices.bit_length() - 1
    distances = []
    for level_idx in range(levels):
        stride = 2**level_idx
        if 2 * stride == seq_devices:
            distances.append(stride)
        else:
            distances.extend([stride, -stride])
    return distances


def node_plan(position, seq_index, dev_rows, capacity, seq_devices):
    own_position = lax.dynamic_slice_in_dim(position, seq_index * dev_rows, dev_rows)
    target_dev = own_position // dev_rows
    dest_hits = (target_dev[:, None] == jnp.arange(seq_devices, dtype=jnp.int32)[None, :]).astype(
        jnp.int32
    )
    send_rank = jnp.sum((jnp.cumsum(dest_hits, axis=0) - dest_hits) * dest_hits, axis=1)
    send_index = target_dev * capacity + send_rank
    layout = position.reshape(seq_devices, dev_rows)
    arriving = (layout // dev_rows == seq_index).astype(jnp.int32)
    arrive_rank = jnp.cumsum(arriving, axis=1) - arriving
    source_index = jnp.arange(seq_devices, dtype=jnp.int32)[:, None] * capacity + arrive_rank
    del source_index
    total = position.shape[0]
    wanted = seq_index * dev_rows + jnp.arange(dev_rows, dtype=jnp.int32)
    slot_node = jnp.sum(
        jnp.where(
            position[None, :] == wanted[:, None], jnp.arange(total, dtype=jnp.int32)[None, :], 0
        ),
        axis=1,
    )
    source_for_slot = slot_node // dev_rows * capacity + arrive_rank.reshape(-1)[slot_node]
    return (send_index, source_for_slot)


def attention_forward(queries, keyval_all, selected):
    query_heads = split_heads(queries)
    key_heads, value_heads = listed_heads(keyval_all, selected)
    scores = (
        jnp.einsum("aihd,akjhd->haikj", query_heads, key_heads, preferred_element_type=jnp.float32)
        * 0.125
    )
    largest = jnp.max(scores, axis=(3, 4), keepdims=True)
    totals = jnp.sum(jnp.exp(scores - largest), axis=(3, 4), keepdims=True)
    log_totals = largest + jnp.log(totals)
    attn_probs = jnp.exp(scores - log_totals).astype(jnp.bfloat16)
    result = jnp.einsum(
        "haikj,akjhd->aihd", attn_probs, value_heads, preferred_element_type=jnp.float32
    )
    return (result.astype(jnp.bfloat16).reshape(queries.shape[0], D), log_totals)


def attention_backward(queries, keyval_all, selected, attn_out, log_totals, grad_attn):
    query_heads = split_heads(queries)
    key_heads, value_heads = listed_heads(keyval_all, selected)
    out_heads = split_heads(attn_out)
    grad_heads = split_heads(grad_attn)
    scores = (
        jnp.einsum("aihd,akjhd->haikj", query_heads, key_heads, preferred_element_type=jnp.float32)
        * 0.125
    )
    attn_exact = jnp.exp(scores - log_totals)
    attn_probs = attn_exact.astype(jnp.bfloat16)
    grad_probs = jnp.einsum(
        "aihd,akjhd->haikj", grad_heads, value_heads, preferred_element_type=jnp.float32
    )
    row_dots = jnp.einsum(
        "aihd,aihd->hai", grad_heads, out_heads, preferred_element_type=jnp.float32
    )[..., None, None]
    grad_scores = (attn_exact * (grad_probs - row_dots) * 0.125).astype(jnp.bfloat16)
    grad_query = jnp.einsum(
        "haikj,akjhd->aihd", grad_scores, key_heads, preferred_element_type=jnp.float32
    )
    grad_keys = jnp.einsum(
        "haikj,aihd->akjhd", grad_scores, query_heads, preferred_element_type=jnp.float32
    )
    grad_values = jnp.einsum(
        "haikj,aihd->akjhd", attn_probs, grad_heads, preferred_element_type=jnp.float32
    )
    block_shape = grad_keys.shape[:3] + (D,)
    grad_picked = jnp.concatenate(
        [grad_keys.reshape(block_shape), grad_values.reshape(block_shape)], axis=-1
    )
    total_rows = keyval_all.shape[0]
    grad_keyval = (
        jnp.zeros((total_rows // BLK, BLK, 2 * D), jnp.float32).at[selected].add(grad_picked)
    )
    return (
        grad_query.astype(jnp.bfloat16).reshape(queries.shape[0], D),
        grad_keyval.reshape(total_rows, 2 * D),
    )


def ring_position(kind):
    seq_index = lax.axis_index("seq")
    if kind == "x":
        return seq_index // 2 % 4
    if kind == "y":
        return seq_index // 8
    return lax.axis_index("dp")


def ring_send(rows, kind, shift):
    if kind == "z":
        size = lax.axis_size("dp")
        return lax.ppermute(rows, "dp", [(i, (i + shift) % size) for i in range(size)])
    size = lax.axis_size("seq")
    if kind == "x":
        move = lambda i: i - i // 2 % 4 * 2 + (i // 2 % 4 + shift) % 4 * 2
    else:
        move = lambda i: (i // 8 + shift) % 4 * 8 + i % 8
    return lax.ppermute(rows, "seq", [(i, move(i)) for i in range(size)])


def in_member_order(pieces, position):
    count = len(pieces)
    placed = jnp.zeros((count,) + pieces[0].shape, pieces[0].dtype)
    for offset, piece in enumerate(pieces):
        placed = lax.dynamic_update_index_in_dim(placed, piece, (position - offset) % count, 0)
    return placed


def scatter_stage(rows, gains, kind):
    position = ring_position(kind)
    part = rows.shape[0] // 4
    chunks = rows.reshape(4, part, rows.shape[1])
    total = lax.dynamic_index_in_dim(chunks, position, keepdims=False)
    gains_sent = None if gains is None else gains.astype(jnp.bfloat16)
    gains_got = [gains_sent]
    for shift in (1, 2, 3):
        piece = lax.dynamic_index_in_dim(chunks, (position + shift) % 4, keepdims=False)
        message = piece.astype(jnp.bfloat16)
        if gains is not None:
            message = jnp.concatenate([message, gains_sent], axis=0)
        got = ring_send(message, kind, shift)
        total = total + got[:part].astype(jnp.float32)
        if gains is not None:
            gains_got.append(got[part:])
    if gains is not None:
        canon = in_member_order(gains_got, position).astype(jnp.float32)
        gains = canon[0] + canon[1] + (canon[2] + canon[3])
    return (total, gains)


def gather_stage(rows, kind):
    position = ring_position(kind)
    pieces = [rows] + [ring_send(rows, kind, shift) for shift in (1, 2, 3)]
    canon = in_member_order(pieces, position)
    return canon.reshape(4 * rows.shape[0], rows.shape[1])


AXIS_ORDERS = (("x", "y", "z"),)


def reduce_everywhere(rows, gains):
    seq_devices = lax.axis_size("seq")
    core = lax.axis_index("seq") % 2
    pairs = [(i, i ^ 1) for i in range(seq_devices)]
    half = rows.shape[0] // 2
    halves = rows.reshape(2, half, rows.shape[1])
    own = lax.dynamic_index_in_dim(halves, core, keepdims=False)
    other = lax.dynamic_index_in_dim(halves, 1 - core, keepdims=False)
    gains_sent = gains.astype(jnp.bfloat16)
    got = lax.ppermute(
        jnp.concatenate([other.astype(jnp.bfloat16), gains_sent], axis=0), "seq", pairs
    )
    summed = own + got[:half].astype(jnp.float32)
    gains = gains_sent.astype(jnp.float32) + got[half:].astype(jnp.float32)
    third = half // len(AXIS_ORDERS)
    done = []
    for part_idx, order in enumerate(AXIS_ORDERS):
        part = summed[part_idx * third : (part_idx + 1) * third]
        part_gains = gains if part_idx == 0 else None
        for kind in order:
            part, part_gains = scatter_stage(part, part_gains, kind)
        if part_idx == 0:
            gains = part_gains
        part = part.astype(jnp.bfloat16)
        for kind in reversed(order):
            part = gather_stage(part, kind)
        done.append(part)
    mine = jnp.concatenate(done, axis=0)
    partner = lax.ppermute(mine, "seq", pairs)
    full = in_member_order([mine, partner], core).reshape(rows.shape)
    return (full.astype(jnp.float32), gains)


def on_device(
    features, curve_pos, pattern, ln1_gain, w_qkv, w_out, ln2_gain, w_up, w_down, out_grad
):
    seq_devices = lax.axis_size("seq")
    seq_index = lax.axis_index("seq")
    dev_rows = features.shape[1]
    capacity = 2 * dev_rows // seq_devices
    blocks_dev = dev_rows // BLK
    position = curve_pos[0]
    send_index, source_for_slot = node_plan(position, seq_index, dev_rows, capacity, seq_devices)
    outgoing = jnp.zeros((seq_devices * capacity, D), jnp.bfloat16).at[send_index].set(features[0])
    arrived = lax.all_to_all(
        outgoing.reshape(seq_devices, capacity, D), "seq", split_axis=0, concat_axis=0, tiled=True
    )
    curve_rows = arrived.reshape(seq_devices * capacity, D)[source_for_slot]
    normed_a, normed1, inverse1 = layer_norm(curve_rows, ln1_gain)
    qkv = jnp.dot(normed_a, w_qkv, preferred_element_type=jnp.float32).astype(jnp.bfloat16)
    queries = qkv[:, :D]
    keyval = qkv[:, D:]
    distances = shift_distances(seq_devices)
    pieces = [keyval]
    for distance in distances:
        pieces.append(from_behind(keyval, "seq", distance))
    keyval_all = jnp.concatenate(pieces, axis=0)
    source_dev = jnp.stack(
        [seq_index] + [(seq_index - distance) % seq_devices for distance in distances]
    )
    key_blocks = (
        source_dev[:, None] * blocks_dev + jnp.arange(blocks_dev, dtype=jnp.int32)[None, :]
    ).reshape(-1)
    own_lists = lax.dynamic_slice_in_dim(pattern[0], seq_index * blocks_dev, blocks_dev, axis=0)
    matches = (own_lists[:, :, None] == key_blocks[None, None, :]).astype(jnp.int32)
    selected = jnp.sum(
        matches * jnp.arange(key_blocks.shape[0], dtype=jnp.int32)[None, None, :], axis=-1
    )
    attn_out, log_totals = attention_forward(queries, keyval_all, selected)
    hidden_res = (
        curve_rows.astype(jnp.float32)
        + jnp.dot(attn_out, w_out, preferred_element_type=jnp.float32)
    ).astype(jnp.bfloat16)
    normed_b, normed2, inverse2 = layer_norm(hidden_res, ln2_gain)
    pre_act = jnp.dot(normed_b, w_up, preferred_element_type=jnp.float32)
    activated = jax.nn.gelu(pre_act, approximate=True).astype(jnp.bfloat16)
    curve_out = (
        hidden_res.astype(jnp.float32)
        + jnp.dot(activated, w_down, preferred_element_type=jnp.float32)
    ).astype(jnp.bfloat16)
    leaving = (
        jnp.zeros((seq_devices * capacity, D), jnp.bfloat16).at[source_for_slot].set(curve_out)
    )
    returned = lax.all_to_all(
        leaving.reshape(seq_devices, capacity, D), "seq", split_axis=0, concat_axis=0, tiled=True
    )
    block_out = returned.reshape(seq_devices * capacity, D)[send_index]
    grad_outgoing = (
        jnp.zeros((seq_devices * capacity, D), jnp.bfloat16).at[send_index].set(out_grad[0])
    )
    grad_arrived = lax.all_to_all(
        grad_outgoing.reshape(seq_devices, capacity, D),
        "seq",
        split_axis=0,
        concat_axis=0,
        tiled=True,
    )
    grad_curve = grad_arrived.reshape(seq_devices * capacity, D)[source_for_slot]
    grad_pre = gelu_back(pre_act, times_transposed(grad_curve, w_down)).astype(jnp.bfloat16)
    grad_down = inner_rows(activated, grad_curve)
    grad_normed_b = times_transposed(grad_pre, w_up)
    grad_up = inner_rows(normed_b, grad_pre)
    grad_gain2 = jnp.sum(grad_normed_b * normed2, axis=0)
    grad_up, grad_down = lax.psum((grad_up, grad_down), ("seq", "dp"))
    grad_hidden = (
        grad_curve.astype(jnp.float32) + norm_back(grad_normed_b, ln2_gain, normed2, inverse2)
    ).astype(jnp.bfloat16)
    grad_attn = times_transposed(grad_hidden, w_out).astype(jnp.bfloat16)
    grad_out = inner_rows(attn_out, grad_hidden)
    resent = [keyval]
    for distance in distances:
        resent.append(from_behind(keyval, "seq", distance))
    keyval_back = jnp.concatenate(resent, axis=0)
    grad_query, grad_keyval_all = attention_backward(
        queries, keyval_back, selected, attn_out, log_totals, grad_attn
    )
    grad_keyval = grad_keyval_all[:dev_rows]
    for index_pos, distance in enumerate(distances):
        partial_rows = grad_keyval_all[(index_pos + 1) * dev_rows : (index_pos + 2) * dev_rows]
        grad_keyval = grad_keyval + from_behind(
            partial_rows.astype(jnp.bfloat16), "seq", -distance
        ).astype(partial_rows.dtype)
    grad_qkv_rows = jnp.concatenate([grad_query, grad_keyval.astype(jnp.bfloat16)], axis=1)
    grad_normed_a = times_transposed(grad_qkv_rows, w_qkv)
    grad_qkv = inner_rows(normed_a, grad_qkv_rows)
    grad_gain1 = jnp.sum(grad_normed_a * normed1, axis=0)
    grad_curve_in = (
        grad_hidden.astype(jnp.float32) + norm_back(grad_normed_a, ln1_gain, normed1, inverse1)
    ).astype(jnp.bfloat16)
    grad_leaving = (
        jnp.zeros((seq_devices * capacity, D), jnp.bfloat16).at[source_for_slot].set(grad_curve_in)
    )
    grad_returned = lax.all_to_all(
        grad_leaving.reshape(seq_devices, capacity, D),
        "seq",
        split_axis=0,
        concat_axis=0,
        tiled=True,
    )
    input_grad = grad_returned.reshape(seq_devices * capacity, D)[send_index]
    weight_rows = jnp.concatenate(
        [grad_qkv[:, index * D : (index + 1) * D] for index in range(3)] + [grad_out], axis=0
    )
    gain_rows = jnp.zeros((8, D), jnp.float32).at[0].set(grad_gain1).at[1].set(grad_gain2)
    weight_rows, gain_rows = reduce_everywhere(weight_rows, gain_rows)
    grad_qkv = jnp.concatenate(
        [weight_rows[index * D : (index + 1) * D] for index in range(3)], axis=1
    )
    grad_out = weight_rows[3 * D :]
    grad_gain1 = gain_rows[0]
    grad_gain2 = gain_rows[1]
    return (
        block_out[None],
        input_grad[None],
        grad_qkv,
        grad_out,
        grad_up,
        grad_down,
        grad_gain1,
        grad_gain2,
    )


def solution(mesh):
    return jax.shard_map(
        on_device,
        mesh=mesh,
        in_specs=(
            P("dp", "seq", None),
            P("dp", None),
            P("dp", None, None),
            P(),
            P(),
            P(),
            P(),
            P(),
            P(),
            P("dp", "seq", None),
        ),
        out_specs=(P("dp", "seq", None), P("dp", "seq", None), P(), P(), P(), P(), P(), P()),
        check_vma=False,
    )
```

profile of v0, /device:TPU:1, one launch (start us, length us, event | category | flops | bytes accessed | tf_op | source)
XLA Modules:
  0.0 500.6 jit_solution(13440220894397012022)
XLA Ops:
  14.5 8.6 %all-to-all-start = ((bf16[32,16,512]{2,1,0:T(8,128)(2,1)}), bf16[32,16,512]{2,1,0:T(8,128)(2,1)S(1)}, u32[]{:S(2)}, u32[]{:S(2)}) async-start(bf16[32,16,512]{2,1,0:T(8,128)(2,1)} %bitcast.16), calls=%async_computation | async-start | bytes 1048576 | tf_op jit(solution)/shard_map/all_to_all | solution.py:262
  55.9 5.1 %collective-permute-start.5 = (bf16[256,1024]{1,0:T(8,128)(2,1)}, bf16[256,1024]{1,0:T(8,128)(2,1)S(1)}, u32[]{:S(2)}, u32[]{:S(2)}) collective-permute-start(bf16[256,1024]{1,0:T(8,128)(2,1)} %get-tuple-element.69), channel_id=1, source_target_pairs={{0,112},{4,116},{8,120},{12,124},{16,0},{20,4},{24,8},{28,12},{32,... | collective-permute-start | bytes 1572872 | tf_op jit(solution)/shard_map/ppermute | solution.py:15
  73.9 19.9 %collective-permute-start.8 = (bf16[256,1024]{1,0:T(8,128)(2,1)}, bf16[256,1024]{1,0:T(8,128)(2,1)S(1)}, u32[]{:S(2)}, u32[]{:S(2)}) collective-permute-start(bf16[256,1024]{1,0:T(8,128)(2,1)} %get-tuple-element.69), channel_id=1, source_target_pairs={{0,64},{4,68},{8,72},{12,76},{16,80},{20,84},{24,88},{28,92},{32,9... | collective-permute-start | bytes 1572872 | tf_op jit(solution)/shard_map/ppermute | solution.py:15
  100.3 6.1 %collective-permute-done.8 = bf16[256,1024]{1,0:T(8,128)(2,1)S(1)} collective-permute-done((bf16[256,1024]{1,0:T(8,128)(2,1)}, bf16[256,1024]{1,0:T(8,128)(2,1)S(1)}, u32[]{:S(2)}, u32[]{:S(2)}) %collective-permute-start.8) | collective-permute-done | bytes 524320 | tf_op jit(solution)/shard_map/ppermute | solution.py:15
  107.2 5.3 %gather_fusion.2 = bf16[16,128,1024]{2,1,0:T(8,128)(2,1)} fusion(bf16[20,128,1024]{2,1,0:T(8,128)(2,1)} %bitcast.311, s32[1024]{0:T(1024)S(1)} %pad_clamp_fusion.1), kind=kCustom, calls=%fused_computation.2 | custom fusion | bytes 8388672 | tf_op jit(solution)/shard_map/gather | solution.py:57
  112.5 6.4 %copy.98 = bf16[16,128,1024]{1,2,0:T(8,128)(2,1)} copy(bf16[16,128,1024]{2,1,0:T(8,128)(2,1)} %gather_fusion.2) | data formatting | bytes 8388608 | tf_op jit(solution)/shard_map/gather | solution.py:57
  134.6 5.2 %fusion.9 = f32[2,8,128,8,64]{2,4,1,3,0:T(8,128)S(1)} fusion(bf16[2,128,8,64,1]{1,0,3,2,4:T(2,128)(2,1)S(1)} %bitcast.316, f32[8,2,128,8,128]{2,4,3,1,0:T(8,128)} %copy-done.2, f32[8,2,128]{2,1,0:T(2,128)S(1)} %bitcast.351), kind=kOutput, calls=%fused_computation.31 | convolution fusion | flops 274726912 | bytes 12853248 | tf_op jit(solution)/shard_map/haikj,aihd->akjhd/dot_general | solution.py:140
  139.8 5.5 %multiply_convert_fusion = bf16[8,2,128,8,128]{2,4,3,1,0:T(8,128)(2,1)S(1)} fusion(f32[8,2,128,8,128]{2,4,3,1,0:T(8,128)} %copy-done.2, f32[8,2,128]{2,1,0:T(2,128)S(1)} %copy.131, f32[8,2,128]{2,1,0:T(2,128)S(1)} %bitcast.352, bf16[2,8,128,8,64]{2,4,3,1,0:T(8,128)(2,1)S(1)} %bitcast.322, bf16[2,128,8,64,1]{1,0,3,2,4:T(2,128)(2,1)S(1)} %bitcast.317), kind=kOutput, calls=%fused_computation.12 | convolution fusion | flops 281018368 | bytes 14958592 | tf_op jit(solution)/shard_map/aihd,akjhd->haikj/dot_general | solution.py:127
  152.0 9.3 %copy.118 = f32[16,128,1024]{2,1,0:T(8,128)} copy(f32[16,128,1024]{1,2,0:T(8,128)} %bitcast.297) | data formatting | bytes 16777216 | tf_op jit(solution)/shard_map/concatenate | solution.py:144
  161.2 5.3 %broadcast_in_dim.151 = f32[20,128,1024]{2,1,0:T(8,128)} broadcast(f32[]{:T(128)} %constant.469.clone.1), dimensions={} | broadcast | bytes 10485764 | tf_op jit(solution)/shard_map/broadcast_in_dim | solution.py:149
  166.6 18.3 %scatter_fusion = f32[20,128,1024]{2,1,0:T(8,128)} fusion(f32[20,128,1024]{2,1,0:T(8,128)} %broadcast_in_dim.151, s32[16]{0:T(128)S(1)} %reshape.628, f32[16,128,1024]{2,1,0:T(8,128)} %copy.118), kind=kCustom, calls=%fused_computation.9 | custom fusion | flops 2097152 | bytes 25165888 | tf_op jit(solution)/shard_map/scatter-add | solution.py:149
  192.0 5.1 %collective-permute-start.11 = (bf16[256,1024]{1,0:T(8,128)(2,1)}, bf16[256,1024]{1,0:T(8,128)(2,1)}, u32[]{:S(2)}, u32[]{:S(2)}) collective-permute-start(bf16[256,1024]{1,0:T(8,128)(2,1)} %bitcast.59), channel_id=1, source_target_pairs={{0,120},{4,124},{8,0},{12,4},{16,8},{20,12},{24,16},{28,20},{32,24... | collective-permute-start | bytes 1572872 | tf_op jit(solution)/shard_map/ppermute | solution.py:15
  205.4 26.0 %collective-permute-done.11 = bf16[256,1024]{1,0:T(8,128)(2,1)} collective-permute-done((bf16[256,1024]{1,0:T(8,128)(2,1)}, bf16[256,1024]{1,0:T(8,128)(2,1)}, u32[]{:S(2)}, u32[]{:S(2)}) %collective-permute-start.11) | collective-permute-done | bytes 524320 | tf_op jit(solution)/shard_map/ppermute | solution.py:15
  231.4 6.6 %collective-permute-done.12 = bf16[256,1024]{1,0:T(8,128)(2,1)} collective-permute-done((bf16[256,1024]{1,0:T(8,128)(2,1)}, bf16[256,1024]{1,0:T(8,128)(2,1)}, u32[]{:S(2)}, u32[]{:S(2)}) %collective-permute-start.12) | collective-permute-done | bytes 524320 | tf_op jit(solution)/shard_map/ppermute | solution.py:15
  249.2 11.9 %collective-permute-done.17 = bf16[256,1024]{1,0:T(8,128)(2,1)} collective-permute-done((bf16[256,1024]{1,0:T(8,128)(2,1)}, bf16[256,1024]{1,0:T(8,128)(2,1)}, u32[]{:S(2)}, u32[]{:S(2)}) %collective-permute-start.17) | collective-permute-done | bytes 524320 | tf_op jit(solution)/shard_map/ppermute | solution.py:15
  289.4 5.5 %collective-permute-done.20 = bf16[264,512]{1,0:T(8,128)(2,1)S(1)} collective-permute-done((bf16[264,512]{1,0:T(8,128)(2,1)S(1)}, bf16[264,512]{1,0:T(8,128)(2,1)S(1)}, u32[]{:S(2)}, u32[]{:S(2)}) %collective-permute-start.20) | collective-permute-done | bytes 270368 | tf_op jit(solution)/shard_map/ppermute | solution.py:175
  301.8 7.9 %all-to-all-start.1 = ((bf16[32,16,512]{2,1,0:T(8,128)(2,1)}), bf16[32,16,512]{2,1,0:T(8,128)(2,1)S(1)}, u32[]{:S(2)}, u32[]{:S(2)}) async-start(bf16[32,16,512]{2,1,0:T(8,128)(2,1)} %bitcast.38), calls=%async_computation.1 | async-start | bytes 1048576 | tf_op jit(solution)/shard_map/all_to_all | solution.py:301
  314.5 5.4 %collective-permute-done.23 = bf16[72,512]{1,0:T(8,128)(2,1)S(1)} collective-permute-done((bf16[72,512]{1,0:T(8,128)(2,1)S(1)}, bf16[72,512]{1,0:T(8,128)(2,1)S(1)}, u32[]{:S(2)}, u32[]{:S(2)}) %collective-permute-start.23) | collective-permute-done | bytes 73760 | tf_op jit(solution)/shard_map/ppermute | solution.py:175
  343.8 8.7 %all-to-all-start.3 = ((bf16[32,16,512]{2,1,0:T(8,128)(2,1)}), bf16[32,16,512]{2,1,0:T(8,128)(2,1)S(1)}, u32[]{:S(2)}, u32[]{:S(2)}) async-start(bf16[32,16,512]{2,1,0:T(8,128)(2,1)} %bitcast.66), calls=%async_computation.3 | async-start | bytes 1048576 | tf_op jit(solution)/shard_map/all_to_all | solution.py:350
  355.9 8.3 %all-to-all-done.3 = bf16[32,16,512]{2,1,0:T(8,128)(2,1)S(1)} async-done(((bf16[32,16,512]{2,1,0:T(8,128)(2,1)}), bf16[32,16,512]{2,1,0:T(8,128)(2,1)S(1)}, u32[]{:S(2)}, u32[]{:S(2)}) %all-to-all-start.3) | async-done | bytes 524320 | tf_op jit(solution)/shard_map/all_to_all | solution.py:350
  369.4 6.3 %collective-permute-done.35 = bf16[256,512]{1,0:T(8,128)(2,1)S(1)} collective-permute-done((bf16[256,512]{1,0:T(8,128)(2,1)S(1)}, bf16[256,512]{1,0:T(8,128)(2,1)S(1)}, u32[]{:S(2)}, u32[]{:S(2)}) %collective-permute-start.35) | collective-permute-done | bytes 262176 | tf_op jit(solution)/shard_map/ppermute | solution.py:175
  375.7 7.3 %collective-permute-done.36 = bf16[256,512]{1,0:T(8,128)(2,1)S(1)} collective-permute-done((bf16[256,512]{1,0:T(8,128)(2,1)S(1)}, bf16[256,512]{1,0:T(8,128)(2,1)S(1)}, u32[]{:S(2)}, u32[]{:S(2)}) %collective-permute-start.36) | collective-permute-done | bytes 262176 | tf_op jit(solution)/shard_map/ppermute | solution.py:175
  389.9 96.8 %all-reduce.4.cloned.1.call-done = (f32[512,2048]{1,0:T(8,128)}, f32[2048,512]{1,0:T(8,128)}) async-done(((f32[512,2048]{1,0:T(8,128)}, f32[2048,512]{1,0:T(8,128)}), (f32[512,2048]{1,0:T(8,128)}, f32[2048,512]{1,0:T(8,128)})) %all-reduce.4.cloned.1.call-update) | async-done | bytes 8388624 | tf_op jit(solution)/shard_map/psum | solution.py:321
  486.7 4.8 copy.262
  (295 shorter events, 189.6 us)
Async XLA Ops:
  14.5 20.1 %all-to-all-start = ((bf16[32,16,512]{2,1,0:T(8,128)(2,1)}), bf16[32,16,512]{2,1,0:T(8,128)(2,1)S(1)}, u32[]{:S(2)}, u32[]{:S(2)}) async-start(bf16[32,16,512]{2,1,0:T(8,128)(2,1)} %bitcast.16), calls=%async_computation | async-start | bytes 1048576 | tf_op jit(solution)/shard_map/all_to_all | solution.py:262
  34.6 16.2 %all-to-all-start.2 = ((bf16[32,16,512]{2,1,0:T(8,128)(2,1)}), bf16[32,16,512]{2,1,0:T(8,128)(2,1)S(1)}, u32[]{:S(2)}, u32[]{:S(2)}) async-start(bf16[32,16,512]{2,1,0:T(8,128)(2,1)} %bitcast.320), calls=%async_computation.2 | async-start | bytes 1048576 | tf_op jit(solution)/shard_map/all_to_all | solution.py:308
  45.9 17.1 %collective-permute-start.1 = (bf16[256,1024]{1,0:T(8,128)(2,1)}, bf16[256,1024]{1,0:T(8,128)(2,1)}, u32[]{:S(2)}, u32[]{:S(2)}) collective-permute-start(bf16[256,1024]{1,0:T(8,128)(2,1)} %get-tuple-element.69), channel_id=1, source_target_pairs={{0,124},{4,0},{8,4},{12,8},{16,12},{20,16},{24,20},{28,24},{32,28}... | collective-permute-start | bytes 1572872 | tf_op jit(solution)/shard_map/ppermute | solution.py:15
  45.9 23.1 %collective-permute-start.2 = (bf16[256,1024]{1,0:T(8,128)(2,1)}, bf16[256,1024]{1,0:T(8,128)(2,1)}, u32[]{:S(2)}, u32[]{:S(2)}) collective-permute-start(bf16[256,1024]{1,0:T(8,128)(2,1)} %get-tuple-element.69), channel_id=1, source_target_pairs={{0,8},{4,12},{8,16},{12,20},{16,24},{20,28},{24,32},{28,36},{32,40... | collective-permute-start | bytes 1572872 | tf_op jit(solution)/shard_map/ppermute | solution.py:15
  47.2 26.8 %collective-permute-start.3 = (bf16[256,1024]{1,0:T(8,128)(2,1)}, bf16[256,1024]{1,0:T(8,128)(2,1)}, u32[]{:S(2)}, u32[]{:S(2)}) collective-permute-start(bf16[256,1024]{1,0:T(8,128)(2,1)} %get-tuple-element.69), channel_id=1, source_target_pairs={{0,120},{4,124},{8,0},{12,4},{16,8},{20,12},{24,16},{28,20},{32,24... | collective-permute-start | bytes 1572872 | tf_op jit(solution)/shard_map/ppermute | solution.py:15
  50.8 45.0 %collective-permute-start.4 = (bf16[256,1024]{1,0:T(8,128)(2,1)}, bf16[256,1024]{1,0:T(8,128)(2,1)}, u32[]{:S(2)}, u32[]{:S(2)}) collective-permute-start(bf16[256,1024]{1,0:T(8,128)(2,1)} %get-tuple-element.69), channel_id=1, source_target_pairs={{0,16},{4,20},{8,24},{12,28},{16,32},{20,36},{24,40},{28,44},{32,4... | collective-permute-start | bytes 1572872 | tf_op jit(solution)/shard_map/ppermute | solution.py:15
  55.9 41.7 %collective-permute-start.5 = (bf16[256,1024]{1,0:T(8,128)(2,1)}, bf16[256,1024]{1,0:T(8,128)(2,1)S(1)}, u32[]{:S(2)}, u32[]{:S(2)}) collective-permute-start(bf16[256,1024]{1,0:T(8,128)(2,1)} %get-tuple-element.69), channel_id=1, source_target_pairs={{0,112},{4,116},{8,120},{12,124},{16,0},{20,4},{24,8},{28,12},{32,... | collective-permute-start | bytes 1572872 | tf_op jit(solution)/shard_map/ppermute | solution.py:15
  63.0 35.5 %collective-permute-start.6 = (bf16[256,1024]{1,0:T(8,128)(2,1)}, bf16[256,1024]{1,0:T(8,128)(2,1)S(1)}, u32[]{:S(2)}, u32[]{:S(2)}) collective-permute-start(bf16[256,1024]{1,0:T(8,128)(2,1)} %get-tuple-element.69), channel_id=1, source_target_pairs={{0,32},{4,36},{8,40},{12,44},{16,48},{20,52},{24,56},{28,60},{32,6... | collective-permute-start | bytes 1572872 | tf_op jit(solution)/shard_map/ppermute | solution.py:15
  69.0 30.5 %collective-permute-start.7 = (bf16[256,1024]{1,0:T(8,128)(2,1)}, bf16[256,1024]{1,0:T(8,128)(2,1)S(1)}, u32[]{:S(2)}, u32[]{:S(2)}) collective-permute-start(bf16[256,1024]{1,0:T(8,128)(2,1)} %get-tuple-element.69), channel_id=1, source_target_pairs={{0,96},{4,100},{8,104},{12,108},{16,112},{20,116},{24,120},{28,124... | collective-permute-start | bytes 1572872 | tf_op jit(solution)/shard_map/ppermute | solution.py:15
  73.9 32.4 %collective-permute-start.8 = (bf16[256,1024]{1,0:T(8,128)(2,1)}, bf16[256,1024]{1,0:T(8,128)(2,1)S(1)}, u32[]{:S(2)}, u32[]{:S(2)}) collective-permute-start(bf16[256,1024]{1,0:T(8,128)(2,1)} %get-tuple-element.69), channel_id=1, source_target_pairs={{0,64},{4,68},{8,72},{12,76},{16,80},{20,84},{24,88},{28,92},{32,9... | collective-permute-start | bytes 1572872 | tf_op jit(solution)/shard_map/ppermute | solution.py:15
  192.0 39.4 %collective-permute-start.11 = (bf16[256,1024]{1,0:T(8,128)(2,1)}, bf16[256,1024]{1,0:T(8,128)(2,1)}, u32[]{:S(2)}, u32[]{:S(2)}) collective-permute-start(bf16[256,1024]{1,0:T(8,128)(2,1)} %bitcast.59), channel_id=1, source_target_pairs={{0,120},{4,124},{8,0},{12,4},{16,8},{20,12},{24,16},{28,20},{32,24... | collective-permute-start | bytes 1572872 | tf_op jit(solution)/shard_map/ppermute | solution.py:15
  197.2 40.8 %collective-permute-start.12 = (bf16[256,1024]{1,0:T(8,128)(2,1)}, bf16[256,1024]{1,0:T(8,128)(2,1)}, u32[]{:S(2)}, u32[]{:S(2)}) collective-permute-start(bf16[256,1024]{1,0:T(8,128)(2,1)} %bitcast.60), channel_id=1, source_target_pairs={{0,8},{4,12},{8,16},{12,20},{16,24},{20,28},{24,32},{28,36},{32,40... | collective-permute-start | bytes 1572872 | tf_op jit(solution)/shard_map/ppermute | solution.py:15
  197.2 40.8 %collective-permute-start.13 = (bf16[256,1024]{1,0:T(8,128)(2,1)}, bf16[256,1024]{1,0:T(8,128)(2,1)}, u32[]{:S(2)}, u32[]{:S(2)}) collective-permute-start(bf16[256,1024]{1,0:T(8,128)(2,1)} %bitcast.61), channel_id=1, source_target_pairs={{0,112},{4,116},{8,120},{12,124},{16,0},{20,4},{24,8},{28,12},{32,... | collective-permute-start | bytes 1572872 | tf_op jit(solution)/shard_map/ppermute | solution.py:15
  200.7 45.6 %collective-permute-start.14 = (bf16[256,1024]{1,0:T(8,128)(2,1)}, bf16[256,1024]{1,0:T(8,128)(2,1)}, u32[]{:S(2)}, u32[]{:S(2)}) collective-permute-start(bf16[256,1024]{1,0:T(8,128)(2,1)} %bitcast.334), channel_id=1, source_target_pairs={{0,16},{4,20},{8,24},{12,28},{16,32},{20,36},{24,40},{28,44},{32,4... | collective-permute-start | bytes 1572872 | tf_op jit(solution)/shard_map/ppermute | solution.py:15
  202.4 43.9 %collective-permute-start.15 = (bf16[256,1024]{1,0:T(8,128)(2,1)}, bf16[256,1024]{1,0:T(8,128)(2,1)}, u32[]{:S(2)}, u32[]{:S(2)}) collective-permute-start(bf16[256,1024]{1,0:T(8,128)(2,1)} %bitcast.333), channel_id=1, source_target_pairs={{0,96},{4,100},{8,104},{12,108},{16,112},{20,116},{24,120},{28,124... | collective-permute-start | bytes 1572872 | tf_op jit(solution)/shard_map/ppermute | solution.py:15
  231.4 17.8 %collective-permute-start.16 = (bf16[256,1024]{1,0:T(8,128)(2,1)}, bf16[256,1024]{1,0:T(8,128)(2,1)}, u32[]{:S(2)}, u32[]{:S(2)}) collective-permute-start(bf16[256,1024]{1,0:T(8,128)(2,1)} %bitcast.332), channel_id=1, source_target_pairs={{0,32},{4,36},{8,40},{12,44},{16,48},{20,52},{24,56},{28,60},{32,6... | collective-permute-start | bytes 1572872 | tf_op jit(solution)/shard_map/ppermute | solution.py:15
  238.0 23.0 %collective-permute-start.17 = (bf16[256,1024]{1,0:T(8,128)(2,1)}, bf16[256,1024]{1,0:T(8,128)(2,1)}, u32[]{:S(2)}, u32[]{:S(2)}) collective-permute-start(bf16[256,1024]{1,0:T(8,128)(2,1)} %bitcast.331), channel_id=1, source_target_pairs={{0,64},{4,68},{8,72},{12,76},{16,80},{20,84},{24,88},{28,92},{32,9... | collective-permute-start | bytes 1572872 | tf_op jit(solution)/shard_map/ppermute | solution.py:15
  238.0 23.0 %collective-permute-start.9 = (bf16[256,1024]{1,0:T(8,128)(2,1)}, bf16[256,1024]{1,0:T(8,128)(2,1)}, u32[]{:S(2)}, u32[]{:S(2)}) collective-permute-start(bf16[256,1024]{1,0:T(8,128)(2,1)} %bitcast.330), channel_id=1, source_target_pairs={{0,124},{4,0},{8,4},{12,8},{16,12},{20,16},{24,20},{28,24},{32,28}... | collective-permute-start | bytes 1572872 | tf_op jit(solution)/shard_map/ppermute | solution.py:15
  296.2 18.3 %collective-permute-start.22 = (bf16[72,512]{1,0:T(8,128)(2,1)}, bf16[72,512]{1,0:T(8,128)(2,1)S(1)}, u32[]{:S(2)}, u32[]{:S(2)}) collective-permute-start(bf16[72,512]{1,0:T(8,128)(2,1)} %get-tuple-element.84), channel_id=1, source_target_pairs={{0,32},{4,36},{8,40},{12,44},{16,48},{20,52},{24,56},{28,60},{32,6... | collective-permute-start | bytes 221192 | tf_op jit(solution)/shard_map/ppermute | solution.py:175
  301.8 42.0 %all-to-all-start.1 = ((bf16[32,16,512]{2,1,0:T(8,128)(2,1)}), bf16[32,16,512]{2,1,0:T(8,128)(2,1)S(1)}, u32[]{:S(2)}, u32[]{:S(2)}) async-start(bf16[32,16,512]{2,1,0:T(8,128)(2,1)} %bitcast.38), calls=%async_computation.1 | async-start | bytes 1048576 | tf_op jit(solution)/shard_map/all_to_all | solution.py:301
  309.7 177.0 %all-reduce.4.cloned.1.call-start = ((), (), s32[]{:S(2)}) async-start(), calls=%async_computation.4 | async-start | bytes 16777216 | tf_op jit(solution)/shard_map/psum | solution.py:321
  343.8 20.4 %all-to-all-start.3 = ((bf16[32,16,512]{2,1,0:T(8,128)(2,1)}), bf16[32,16,512]{2,1,0:T(8,128)(2,1)S(1)}, u32[]{:S(2)}, u32[]{:S(2)}) async-start(bf16[32,16,512]{2,1,0:T(8,128)(2,1)} %bitcast.66), calls=%async_computation.3 | async-start | bytes 1048576 | tf_op jit(solution)/shard_map/all_to_all | solution.py:350
  352.6 16.7 %collective-permute-start.34 = (bf16[256,512]{1,0:T(8,128)(2,1)S(1)}, bf16[256,512]{1,0:T(8,128)(2,1)S(1)}, u32[]{:S(2)}, u32[]{:S(2)}) collective-permute-start(bf16[256,512]{1,0:T(8,128)(2,1)S(1)} %bitcast.326), channel_id=1, source_target_pairs={{0,8},{4,12},{8,16},{12,20},{16,24},{20,28},{24,0},{28,4},{32,40},... | collective-permute-start | bytes 786440 | tf_op jit(solution)/shard_map/ppermute | solution.py:175
  367.0 16.0 %collective-permute-start.36 = (bf16[256,512]{1,0:T(8,128)(2,1)S(1)}, bf16[256,512]{1,0:T(8,128)(2,1)S(1)}, u32[]{:S(2)}, u32[]{:S(2)}) collective-permute-start(bf16[256,512]{1,0:T(8,128)(2,1)S(1)} %bitcast.328), channel_id=1, source_target_pairs={{0,24},{4,28},{8,0},{12,4},{16,8},{20,12},{24,16},{28,20},{32,56},... | collective-permute-start | bytes 786440 | tf_op jit(solution)/shard_map/ppermute | solution.py:175
  (52 other events, 566.6 us)
Sparse Core Ops, SparseCore 0:
  316.4 170.2 all-reduce.3
where the time goes:
time: 511 us; the launch traced here: 501 us
  waiting for transfers between devices  205 us (40%)
  starting transfers between devices  102 us (20%)
  local copies, waits for them, and re-layouts  86.5 us (17%)
  other arithmetic  50 us (10%)
  matrix products  42.6 us (8%)
  between operations  15.3 us (3%)
    psum x1, waiting for transfers between devices, on_device(): grad_up, grad_down = lax.psum((grad_up, grad_down), ('seq', 'dp'))  96.8 us
    ppermute x18, waiting for transfers between devices, from_behind(): lax.ppermute(x, axis, [(i, (i + by) % length) for i in range(length)])  57.8 us
    ppermute x18, starting transfers between devices, from_behind(): lax.ppermute(x, axis, [(i, (i + by) % length) for i in range(length)])  46.6 us
    ppermute x12, waiting for transfers between devices, ring_send(): return lax.ppermute(rows, 'seq', [(i, move(i)) for i in range(size)])  31.1 us
    unnamed x74, local copies, waits for them, and re-layouts  25.1 us
    scatter-add x1, other arithmetic, attention_backward(): jnp.zeros((total_rows // BLK, BLK, 2 * D), jnp.float32).at[selected]  18.3 us
    ppermute x12, starting transfers between devices, ring_send(): return lax.ppermute(rows, 'seq', [(i, move(i)) for i in range(size)])  15.9 us
    gather x2, local copies, waits for them, and re-layouts, listed_heads(): picked = blocks[selected]  11.7 us
  transfers between devices with their start and end apart: 43, of which 23 were waited for; matrix products, arithmetic and copies ran while one was open for 13% of the time, Pallas kernels for 0%

commit v1 on v0

--- a/solution.py
+++ b/solution.py
@@ -318,7 +318,7 @@
     grad_normed_b = times_transposed(grad_pre, w_up)
     grad_up = inner_rows(normed_b, grad_pre)
     grad_gain2 = jnp.sum(grad_normed_b * normed2, axis=0)
-    grad_up, grad_down = lax.psum((grad_up, grad_down), ("seq", "dp"))
+    grad_up, grad_down = lax.psum(lax.psum((grad_up, grad_down), "seq"), "dp")
     grad_hidden = (
         grad_curve.astype(jnp.float32) + norm_back(grad_normed_b, ln2_gain, normed2, inverse2)
     ).astype(jnp.bfloat16)

time: 511 us -> 569 us (1.11)
  waiting for transfers between devices: 205 us -> 256 us
  local copies, waits for them, and re-layouts: 86.5 us -> 93.4 us
    psum x1 -> x2, waiting for transfers between devices: 96.8 us -> 147 us  [on_device(): grad_up, grad_down = lax.psum(lax.psum((grad_up, grad_down), 'seq'), 'dp')]
    unnamed x74 -> x82, local copies, waits for them, and re-layouts: 25.1 us -> 29.6 us
  transfers between devices with their start and end apart: 43 -> 44, of which waited for: 23 -> 24; matrix products, arithmetic and copies ran while one was open for 13% -> 14% of each run, Pallas kernels for 0% -> 0%
where the time goes in v1:
time: 569 us; the launch traced here: 559 us
  waiting for transfers between devices  256 us (45%)
  starting transfers between devices  98.9 us (17%)
  local copies, waits for them, and re-layouts  93.4 us (16%)
  other arithmetic  53.4 us (9%)
  matrix products  41.2 us (7%)
  between operations  15.3 us (3%)
    psum x2, waiting for transfers between devices, on_device(): grad_up, grad_down = lax.psum(lax.psum((grad_up, grad_down), 'seq'), 'dp')  147 us
    ppermute x18, waiting for transfers between devices, from_behind(): lax.ppermute(x, axis, [(i, (i + by) % length) for i in range(length)])  56.6 us
    ppermute x18, starting transfers between devices, from_behind(): lax.ppermute(x, axis, [(i, (i + by) % length) for i in range(length)])  44.1 us
    ppermute x12, waiting for transfers between devices, ring_send(): return lax.ppermute(rows, 'seq', [(i, move(i)) for i in range(size)])  31.5 us
    unnamed x82, local copies, waits for them, and re-layouts  29.6 us
    scatter-add x1, other arithmetic, attention_backward(): jnp.zeros((total_rows // BLK, BLK, 2 * D), jnp.float32).at[selected]  18.4 us
    ppermute x12, starting transfers between devices, ring_send(): return lax.ppermute(rows, 'seq', [(i, move(i)) for i in range(size)])  15.9 us
    gather x2, local copies, waits for them, and re-layouts, listed_heads(): picked = blocks[selected]  11.7 us
  transfers between devices with their start and end apart: 44, of which 24 were waited for; matrix products, arithmetic and copies ran while one was open for 14% of the time, Pallas kernels for 0%

profile of v1, /device:TPU:1, one launch (start us, length us, event | category | flops | bytes accessed | tf_op | source)
XLA Modules:
  0.0 558.7 jit_solution(3144665921816767872)
XLA Ops:
  14.5 8.6 %all-to-all-start = ((bf16[32,16,512]{2,1,0:T(8,128)(2,1)}), bf16[32,16,512]{2,1,0:T(8,128)(2,1)S(1)}, u32[]{:S(2)}, u32[]{:S(2)}) async-start(bf16[32,16,512]{2,1,0:T(8,128)(2,1)} %bitcast.16), calls=%async_computation | async-start | bytes 1048576 | tf_op jit(solution)/shard_map/all_to_all | solution.py:262
  56.0 5.1 collective-permute-start.5
  74.1 19.8 %collective-permute-start.8 = (bf16[256,1024]{1,0:T(8,128)(2,1)}, bf16[256,1024]{1,0:T(8,128)(2,1)S(1)}, u32[]{:S(2)}, u32[]{:S(2)}) collective-permute-start(bf16[256,1024]{1,0:T(8,128)(2,1)} %get-tuple-element.71), channel_id=1, source_target_pairs={{0,64},{4,68},{8,72},{12,76},{16,80},{20,84},{24,88},{28,92},{32,9... | collective-permute-start | bytes 1572872 | tf_op jit(solution)/shard_map/ppermute | solution.py:15
  100.8 5.7 %collective-permute-done.8 = bf16[256,1024]{1,0:T(8,128)(2,1)S(1)} collective-permute-done((bf16[256,1024]{1,0:T(8,128)(2,1)}, bf16[256,1024]{1,0:T(8,128)(2,1)S(1)}, u32[]{:S(2)}, u32[]{:S(2)}) %collective-permute-start.8) | collective-permute-done | bytes 524320 | tf_op jit(solution)/shard_map/ppermute | solution.py:15
  107.4 5.3 gather_fusion.2
  112.7 6.4 %copy.98 = bf16[16,128,1024]{1,2,0:T(8,128)(2,1)} copy(bf16[16,128,1024]{2,1,0:T(8,128)(2,1)} %gather_fusion.2) | data formatting | bytes 8388608 | tf_op jit(solution)/shard_map/gather | solution.py:57
  134.8 5.2 fusion.9
  140.0 5.4 multiply_convert_fusion
  152.1 9.3 %copy.118 = f32[16,128,1024]{2,1,0:T(8,128)} copy(f32[16,128,1024]{1,2,0:T(8,128)} %bitcast.297) | data formatting | bytes 16777216 | tf_op jit(solution)/shard_map/concatenate | solution.py:144
  161.4 5.3 broadcast_in_dim.151
  166.8 18.4 %scatter_fusion = f32[20,128,1024]{2,1,0:T(8,128)} fusion(f32[20,128,1024]{2,1,0:T(8,128)} %broadcast_in_dim.151, s32[16]{0:T(128)S(1)} %reshape.628, f32[16,128,1024]{2,1,0:T(8,128)} %copy.118), kind=kCustom, calls=%fused_computation.9 | custom fusion | flops 2097152 | bytes 25165888 | tf_op jit(solution)/shard_map/scatter-add | solution.py:149
  212.1 19.5 %collective-permute-done.11 = bf16[256,1024]{1,0:T(8,128)(2,1)} collective-permute-done((bf16[256,1024]{1,0:T(8,128)(2,1)}, bf16[256,1024]{1,0:T(8,128)(2,1)}, u32[]{:S(2)}, u32[]{:S(2)}) %collective-permute-start.11) | collective-permute-done | bytes 524320 | tf_op jit(solution)/shard_map/ppermute | solution.py:15
  231.6 6.6 %collective-permute-done.12 = bf16[256,1024]{1,0:T(8,128)(2,1)} collective-permute-done((bf16[256,1024]{1,0:T(8,128)(2,1)}, bf16[256,1024]{1,0:T(8,128)(2,1)}, u32[]{:S(2)}, u32[]{:S(2)}) %collective-permute-start.12) | collective-permute-done | bytes 524320 | tf_op jit(solution)/shard_map/ppermute | solution.py:15
  244.2 5.2 collective-permute-done.16
  249.4 14.7 %collective-permute-done.17 = bf16[256,1024]{1,0:T(8,128)(2,1)} collective-permute-done((bf16[256,1024]{1,0:T(8,128)(2,1)}, bf16[256,1024]{1,0:T(8,128)(2,1)}, u32[]{:S(2)}, u32[]{:S(2)}) %collective-permute-start.17) | collective-permute-done | bytes 524320 | tf_op jit(solution)/shard_map/ppermute | solution.py:15
  288.4 6.4 %collective-permute-done.19 = bf16[264,512]{1,0:T(8,128)(2,1)} collective-permute-done((bf16[264,512]{1,0:T(8,128)(2,1)}, bf16[264,512]{1,0:T(8,128)(2,1)}, u32[]{:S(2)}, u32[]{:S(2)}) %collective-permute-start.19) | collective-permute-done | bytes 270368 | tf_op jit(solution)/shard_map/ppermute | solution.py:175
  295.4 5.4 collective-permute-done.20
  302.2 77.5 %all-reduce.6.cloned.1.call-done = (f32[512,2048]{1,0:T(8,128)}, f32[2048,512]{1,0:T(8,128)}) async-done(((f32[512,2048]{1,0:T(8,128)}, f32[2048,512]{1,0:T(8,128)}), (f32[512,2048]{1,0:T(8,128)}, f32[2048,512]{1,0:T(8,128)})) %all-reduce.6.cloned.1.call-update) | async-done | bytes 8388624 | tf_op jit(solution)/shard_map/psum | solution.py:321
  389.5 7.4 %all-to-all-start.1 = ((bf16[32,16,512]{2,1,0:T(8,128)(2,1)}), bf16[32,16,512]{2,1,0:T(8,128)(2,1)S(1)}, u32[]{:S(2)}, u32[]{:S(2)}) async-start(bf16[32,16,512]{2,1,0:T(8,128)(2,1)} %bitcast.38), calls=%async_computation.1 | async-start | bytes 1048576 | tf_op jit(solution)/shard_map/all_to_all | solution.py:301
  400.7 6.3 %collective-permute-done.23 = bf16[72,512]{1,0:T(8,128)(2,1)S(1)} collective-permute-done((bf16[72,512]{1,0:T(8,128)(2,1)S(1)}, bf16[72,512]{1,0:T(8,128)(2,1)S(1)}, u32[]{:S(2)}, u32[]{:S(2)}) %collective-permute-start.23) | collective-permute-done | bytes 73760 | tf_op jit(solution)/shard_map/ppermute | solution.py:175
  432.5 8.6 %all-to-all-start.3 = ((bf16[32,16,512]{2,1,0:T(8,128)(2,1)}), bf16[32,16,512]{2,1,0:T(8,128)(2,1)S(1)}, u32[]{:S(2)}, u32[]{:S(2)}) async-start(bf16[32,16,512]{2,1,0:T(8,128)(2,1)} %bitcast.66), calls=%async_computation.3 | async-start | bytes 1048576 | tf_op jit(solution)/shard_map/all_to_all | solution.py:350
  444.5 8.3 %all-to-all-done.3 = bf16[32,16,512]{2,1,0:T(8,128)(2,1)S(1)} async-done(((bf16[32,16,512]{2,1,0:T(8,128)(2,1)}), bf16[32,16,512]{2,1,0:T(8,128)(2,1)S(1)}, u32[]{:S(2)}, u32[]{:S(2)}) %all-to-all-start.3) | async-done | bytes 524320 | tf_op jit(solution)/shard_map/all_to_all | solution.py:350
  457.6 6.1 %collective-permute-done.35 = bf16[256,512]{1,0:T(8,128)(2,1)S(1)} collective-permute-done((bf16[256,512]{1,0:T(8,128)(2,1)S(1)}, bf16[256,512]{1,0:T(8,128)(2,1)S(1)}, u32[]{:S(2)}, u32[]{:S(2)}) %collective-permute-start.35) | collective-permute-done | bytes 262176 | tf_op jit(solution)/shard_map/ppermute | solution.py:175
  475.7 69.1 %all-reduce.8.cloned.1.call-done = (f32[512,2048]{1,0:T(8,128)}, f32[2048,512]{1,0:T(8,128)}) async-done(((f32[512,2048]{1,0:T(8,128)}, f32[2048,512]{1,0:T(8,128)}), (f32[512,2048]{1,0:T(8,128)}, f32[2048,512]{1,0:T(8,128)})) %all-reduce.8.cloned.1.call-update) | async-done | bytes 8388624 | tf_op jit(solution)/shard_map/psum | solution.py:321
  (306 shorter events, 207.8 us)
Async XLA Ops:
  14.5 20.1 %all-to-all-start = ((bf16[32,16,512]{2,1,0:T(8,128)(2,1)}), bf16[32,16,512]{2,1,0:T(8,128)(2,1)S(1)}, u32[]{:S(2)}, u32[]{:S(2)}) async-start(bf16[32,16,512]{2,1,0:T(8,128)(2,1)} %bitcast.16), calls=%async_computation | async-start | bytes 1048576 | tf_op jit(solution)/shard_map/all_to_all | solution.py:262
  38.6 341.1 %all-reduce.6.cloned.1.call-start = ((), (), s32[]{:S(2)}) async-start(), calls=%async_computation.4 | async-start | bytes 16777216 | tf_op jit(solution)/shard_map/psum | solution.py:321
  45.9 17.1 %collective-permute-start.1 = (bf16[256,1024]{1,0:T(8,128)(2,1)}, bf16[256,1024]{1,0:T(8,128)(2,1)}, u32[]{:S(2)}, u32[]{:S(2)}) collective-permute-start(bf16[256,1024]{1,0:T(8,128)(2,1)} %get-tuple-element.71), channel_id=1, source_target_pairs={{0,124},{4,0},{8,4},{12,8},{16,12},{20,16},{24,20},{28,24},{32,28}... | collective-permute-start | bytes 1572872 | tf_op jit(solution)/shard_map/ppermute | solution.py:15
  45.9 23.1 %collective-permute-start.2 = (bf16[256,1024]{1,0:T(8,128)(2,1)}, bf16[256,1024]{1,0:T(8,128)(2,1)}, u32[]{:S(2)}, u32[]{:S(2)}) collective-permute-start(bf16[256,1024]{1,0:T(8,128)(2,1)} %get-tuple-element.71), channel_id=1, source_target_pairs={{0,8},{4,12},{8,16},{12,20},{16,24},{20,28},{24,32},{28,36},{32,40... | collective-permute-start | bytes 1572872 | tf_op jit(solution)/shard_map/ppermute | solution.py:15
  47.2 26.9 %collective-permute-start.3 = (bf16[256,1024]{1,0:T(8,128)(2,1)}, bf16[256,1024]{1,0:T(8,128)(2,1)}, u32[]{:S(2)}, u32[]{:S(2)}) collective-permute-start(bf16[256,1024]{1,0:T(8,128)(2,1)} %get-tuple-element.71), channel_id=1, source_target_pairs={{0,120},{4,124},{8,0},{12,4},{16,8},{20,12},{24,16},{28,20},{32,24... | collective-permute-start | bytes 1572872 | tf_op jit(solution)/shard_map/ppermute | solution.py:15
  50.8 45.0 %collective-permute-start.4 = (bf16[256,1024]{1,0:T(8,128)(2,1)}, bf16[256,1024]{1,0:T(8,128)(2,1)}, u32[]{:S(2)}, u32[]{:S(2)}) collective-permute-start(bf16[256,1024]{1,0:T(8,128)(2,1)} %get-tuple-element.71), channel_id=1, source_target_pairs={{0,16},{4,20},{8,24},{12,28},{16,32},{20,36},{24,40},{28,44},{32,4... | collective-permute-start | bytes 1572872 | tf_op jit(solution)/shard_map/ppermute | solution.py:15
  56.0 41.7 %collective-permute-start.5 = (bf16[256,1024]{1,0:T(8,128)(2,1)}, bf16[256,1024]{1,0:T(8,128)(2,1)S(1)}, u32[]{:S(2)}, u32[]{:S(2)}) collective-permute-start(bf16[256,1024]{1,0:T(8,128)(2,1)} %get-tuple-element.71), channel_id=1, source_target_pairs={{0,112},{4,116},{8,120},{12,124},{16,0},{20,4},{24,8},{28,12},{32,... | collective-permute-start | bytes 1572872 | tf_op jit(solution)/shard_map/ppermute | solution.py:15
  63.0 35.5 %collective-permute-start.6 = (bf16[256,1024]{1,0:T(8,128)(2,1)}, bf16[256,1024]{1,0:T(8,128)(2,1)S(1)}, u32[]{:S(2)}, u32[]{:S(2)}) collective-permute-start(bf16[256,1024]{1,0:T(8,128)(2,1)} %get-tuple-element.71), channel_id=1, source_target_pairs={{0,32},{4,36},{8,40},{12,44},{16,48},{20,52},{24,56},{28,60},{32,6... | collective-permute-start | bytes 1572872 | tf_op jit(solution)/shard_map/ppermute | solution.py:15
  69.0 30.9 %collective-permute-start.7 = (bf16[256,1024]{1,0:T(8,128)(2,1)}, bf16[256,1024]{1,0:T(8,128)(2,1)S(1)}, u32[]{:S(2)}, u32[]{:S(2)}) collective-permute-start(bf16[256,1024]{1,0:T(8,128)(2,1)} %get-tuple-element.71), channel_id=1, source_target_pairs={{0,96},{4,100},{8,104},{12,108},{16,112},{20,116},{24,120},{28,124... | collective-permute-start | bytes 1572872 | tf_op jit(solution)/shard_map/ppermute | solution.py:15
  74.1 32.4 %collective-permute-start.8 = (bf16[256,1024]{1,0:T(8,128)(2,1)}, bf16[256,1024]{1,0:T(8,128)(2,1)S(1)}, u32[]{:S(2)}, u32[]{:S(2)}) collective-permute-start(bf16[256,1024]{1,0:T(8,128)(2,1)} %get-tuple-element.71), channel_id=1, source_target_pairs={{0,64},{4,68},{8,72},{12,76},{16,80},{20,84},{24,88},{28,92},{32,9... | collective-permute-start | bytes 1572872 | tf_op jit(solution)/shard_map/ppermute | solution.py:15
  192.4 19.1 %collective-permute-start.10 = (bf16[256,1024]{1,0:T(8,128)(2,1)}, bf16[256,1024]{1,0:T(8,128)(2,1)}, u32[]{:S(2)}, u32[]{:S(2)}) collective-permute-start(bf16[256,1024]{1,0:T(8,128)(2,1)} %bitcast.58), channel_id=1, source_target_pairs={{0,4},{4,8},{8,12},{12,16},{16,20},{20,24},{24,28},{28,32},{32,36}... | collective-permute-start | bytes 1572872 | tf_op jit(solution)/shard_map/ppermute | solution.py:15
  192.4 39.2 %collective-permute-start.11 = (bf16[256,1024]{1,0:T(8,128)(2,1)}, bf16[256,1024]{1,0:T(8,128)(2,1)}, u32[]{:S(2)}, u32[]{:S(2)}) collective-permute-start(bf16[256,1024]{1,0:T(8,128)(2,1)} %bitcast.59), channel_id=1, source_target_pairs={{0,120},{4,124},{8,0},{12,4},{16,8},{20,12},{24,16},{28,20},{32,24... | collective-permute-start | bytes 1572872 | tf_op jit(solution)/shard_map/ppermute | solution.py:15
  197.4 40.8 %collective-permute-start.12 = (bf16[256,1024]{1,0:T(8,128)(2,1)}, bf16[256,1024]{1,0:T(8,128)(2,1)}, u32[]{:S(2)}, u32[]{:S(2)}) collective-permute-start(bf16[256,1024]{1,0:T(8,128)(2,1)} %bitcast.60), channel_id=1, source_target_pairs={{0,8},{4,12},{8,16},{12,20},{16,24},{20,28},{24,32},{28,36},{32,40... | collective-permute-start | bytes 1572872 | tf_op jit(solution)/shard_map/ppermute | solution.py:15
  197.4 40.8 %collective-permute-start.13 = (bf16[256,1024]{1,0:T(8,128)(2,1)}, bf16[256,1024]{1,0:T(8,128)(2,1)}, u32[]{:S(2)}, u32[]{:S(2)}) collective-permute-start(bf16[256,1024]{1,0:T(8,128)(2,1)} %bitcast.61), channel_id=1, source_target_pairs={{0,112},{4,116},{8,120},{12,124},{16,0},{20,4},{24,8},{28,12},{32,... | collective-permute-start | bytes 1572872 | tf_op jit(solution)/shard_map/ppermute | solution.py:15
  206.8 37.5 %collective-permute-start.14 = (bf16[256,1024]{1,0:T(8,128)(2,1)}, bf16[256,1024]{1,0:T(8,128)(2,1)}, u32[]{:S(2)}, u32[]{:S(2)}) collective-permute-start(bf16[256,1024]{1,0:T(8,128)(2,1)} %bitcast.330), channel_id=1, source_target_pairs={{0,16},{4,20},{8,24},{12,28},{16,32},{20,36},{24,40},{28,44},{32,4... | collective-permute-start | bytes 1572872 | tf_op jit(solution)/shard_map/ppermute | solution.py:15
  211.5 32.8 %collective-permute-start.15 = (bf16[256,1024]{1,0:T(8,128)(2,1)}, bf16[256,1024]{1,0:T(8,128)(2,1)}, u32[]{:S(2)}, u32[]{:S(2)}) collective-permute-start(bf16[256,1024]{1,0:T(8,128)(2,1)} %bitcast.63), channel_id=1, source_target_pairs={{0,96},{4,100},{8,104},{12,108},{16,112},{20,116},{24,120},{28,124... | collective-permute-start | bytes 1572872 | tf_op jit(solution)/shard_map/ppermute | solution.py:15
  231.6 17.8 %collective-permute-start.16 = (bf16[256,1024]{1,0:T(8,128)(2,1)}, bf16[256,1024]{1,0:T(8,128)(2,1)}, u32[]{:S(2)}, u32[]{:S(2)}) collective-permute-start(bf16[256,1024]{1,0:T(8,128)(2,1)} %bitcast.64), channel_id=1, source_target_pairs={{0,32},{4,36},{8,40},{12,44},{16,48},{20,52},{24,56},{28,60},{32,6... | collective-permute-start | bytes 1572872 | tf_op jit(solution)/shard_map/ppermute | solution.py:15
  238.2 25.9 %collective-permute-start.17 = (bf16[256,1024]{1,0:T(8,128)(2,1)}, bf16[256,1024]{1,0:T(8,128)(2,1)}, u32[]{:S(2)}, u32[]{:S(2)}) collective-permute-start(bf16[256,1024]{1,0:T(8,128)(2,1)} %bitcast.65), channel_id=1, source_target_pairs={{0,64},{4,68},{8,72},{12,76},{16,80},{20,84},{24,88},{28,92},{32,9... | collective-permute-start | bytes 1572872 | tf_op jit(solution)/shard_map/ppermute | solution.py:15
  238.2 25.9 %collective-permute-start.9 = (bf16[256,1024]{1,0:T(8,128)(2,1)}, bf16[256,1024]{1,0:T(8,128)(2,1)}, u32[]{:S(2)}, u32[]{:S(2)}) collective-permute-start(bf16[256,1024]{1,0:T(8,128)(2,1)} %bitcast.57), channel_id=1, source_target_pairs={{0,124},{4,0},{8,4},{12,8},{16,12},{20,16},{24,20},{28,24},{32,28}... | collective-permute-start | bytes 1572872 | tf_op jit(solution)/shard_map/ppermute | solution.py:15
  242.0 302.8 %all-reduce.8.cloned.1.call-start = ((), (), s32[]{:S(2)}) async-start(), calls=%async_computation.5 | async-start | bytes 16777216 | tf_op jit(solution)/shard_map/psum | solution.py:321
  382.7 18.0 %collective-permute-start.22 = (bf16[72,512]{1,0:T(8,128)(2,1)}, bf16[72,512]{1,0:T(8,128)(2,1)S(1)}, u32[]{:S(2)}, u32[]{:S(2)}) collective-permute-start(bf16[72,512]{1,0:T(8,128)(2,1)} %get-tuple-element.86), channel_id=1, source_target_pairs={{0,32},{4,36},{8,40},{12,44},{16,48},{20,52},{24,56},{28,60},{32,6... | collective-permute-start | bytes 221192 | tf_op jit(solution)/shard_map/ppermute | solution.py:175
  389.5 43.0 %all-to-all-start.1 = ((bf16[32,16,512]{2,1,0:T(8,128)(2,1)}), bf16[32,16,512]{2,1,0:T(8,128)(2,1)S(1)}, u32[]{:S(2)}, u32[]{:S(2)}) async-start(bf16[32,16,512]{2,1,0:T(8,128)(2,1)} %bitcast.38), calls=%async_computation.1 | async-start | bytes 1048576 | tf_op jit(solution)/shard_map/all_to_all | solution.py:301
  432.5 20.3 %all-to-all-start.3 = ((bf16[32,16,512]{2,1,0:T(8,128)(2,1)}), bf16[32,16,512]{2,1,0:T(8,128)(2,1)S(1)}, u32[]{:S(2)}, u32[]{:S(2)}) async-start(bf16[32,16,512]{2,1,0:T(8,128)(2,1)} %bitcast.66), calls=%async_computation.3 | async-start | bytes 1048576 | tf_op jit(solution)/shard_map/all_to_all | solution.py:350
  441.2 16.4 %collective-permute-start.34 = (bf16[256,512]{1,0:T(8,128)(2,1)S(1)}, bf16[256,512]{1,0:T(8,128)(2,1)S(1)}, u32[]{:S(2)}, u32[]{:S(2)}) collective-permute-start(bf16[256,512]{1,0:T(8,128)(2,1)S(1)} %bitcast.326), channel_id=1, source_target_pairs={{0,8},{4,12},{8,16},{12,20},{16,24},{20,28},{24,0},{28,4},{32,40},... | collective-permute-start | bytes 786440 | tf_op jit(solution)/shard_map/ppermute | solution.py:175
  (57 other events, 589.0 us)
Sparse Core Ops, SparseCore 0:
  242.2 137.5 all-reduce.5
  382.5 162.2 all-reduce.7
